TPU v7x, 32 devices: a whole 2x2x4 slice. The times are simulated.
32 devices in a mesh: orb: 16 (over z, x, core), aux: 2 (over y).
Axes of the slice: x: 2, y: 2, z: 4, core: 2. Of those that a mesh axis runs over, the one named last changes fastest.
Arguments:
- three_index: float32 [56, 1024, 2048], P(None, 'aux', 'orb'), may hold values from -0.5 to 0.5
- pair_density: float32 [3136, 3136], P('orb'), as said below
- active_orbitals: int32 [56], replicated, may hold values from 200 to 2047, as said below
- screen_mask: int32 [64, 128], P('aux', 'orb'), may hold values from 0 to 1
- one_density: float32 [56, 56], replicated
- inactive_fock: float32 [2048, 256], P('orb'), may hold values from -6 to 6
- active_fock: float32 [2048, 200], P('orb'), may hold values from -6 to 6
Outputs:
- rotation_gradient: float32 [2048, 256], P(('orb', 'aux'))
Inputs may be any that keep to these rules, and one draw needn't show every extreme that they name: `active_orbitals`: 56 distinct orbital indices. pair_density is symmetric: its entry at (tu, vw) equals that at (vw, tu).
All inputs are finite; a program needn't handle non-finite values.
Results may differ from a plain program's by a relative error of at most 0.0001.
Values sent between devices are 32-bit elements; how exact they have to be, the bound alone decides.
No kernel may reach another device: no remote copies, remote signals or barrier semaphores. Data moves between devices by JAX's collectives and lax.ppermute only.
A program may use at most 128 MiB of HBM per device.

v0:
```python
import jax
import jax.numpy as jnp
from jax import lax
from jax.sharding import PartitionSpec as P


def shards(
    three_index, pair_density, active_orbitals, screen_mask, one_density, inactive_fock, active_fock
):
    highest = lax.Precision.HIGHEST
    act_count = three_index.shape[0]
    slab_count = three_index.shape[1]
    row_count = three_index.shape[2]
    inactive_count = active_fock.shape[1]
    orb_position = lax.axis_index("orb")
    kept_mask = jnp.repeat(
        jnp.repeat(screen_mask.astype(jnp.float32), slab_count // screen_mask.shape[0], axis=0),
        row_count // screen_mask.shape[1],
        axis=1,
    )
    screened = three_index * kept_mask[None]
    global_rows = orb_position * row_count + jnp.arange(row_count, dtype=jnp.int32)
    active_pick = (global_rows[:, None] == active_orbitals[None, :]).astype(jnp.float32)
    partial_pairs = jnp.einsum("wPp,pv->Pvw", screened, active_pick, precision=highest).reshape(
        slab_count, act_count * act_count
    )
    pairs = lax.psum(partial_pairs, "orb")
    column_block = jnp.dot(pairs, pair_density.T, precision=highest)
    half = lax.all_gather(column_block, "orb", axis=1, tiled=True)
    q_partial = jnp.einsum(
        "uPp,Ptu->pt", screened, half.reshape(slab_count, act_count, act_count), precision=highest
    )
    occ_index = jnp.concatenate([jnp.arange(inactive_count, dtype=jnp.int32), active_orbitals])
    row_share = row_count // lax.axis_size("aux")
    aux_offset = lax.axis_index("aux") * row_share
    qmatrix = lax.psum(q_partial, "aux")
    inactive_cols = 2.0 * (inactive_fock[:, :inactive_count] + active_fock)
    active_cols = (
        jnp.dot(inactive_fock[:, inactive_count:], one_density, precision=highest) + qmatrix
    )
    fock = jnp.concatenate([inactive_cols, active_cols], axis=1)
    occ_pick = (global_rows[:, None] == occ_index[None, :]).astype(jnp.float32)
    occupied = lax.psum(jnp.dot(occ_pick.T, fock, precision=highest), "orb")
    fock_mine = lax.dynamic_slice_in_dim(fock, aux_offset, row_share, 0)
    pick_mine = lax.dynamic_slice_in_dim(occ_pick, aux_offset, row_share, 0)
    transposed = jnp.dot(pick_mine, occupied.T, precision=highest)
    return 2.0 * (fock_mine - transposed)


def solution(mesh):
    in_specs = (
        P(None, "aux", "orb"),
        P("orb", None),
        P(),
        P("aux", "orb"),
        P(),
        P("orb", None),
        P("orb", None),
    )
    out_specs = P(("orb", "aux"), None)
    return jax.shard_map(shards, mesh=mesh, in_specs=in_specs, out_specs=out_specs, check_vma=False)
```

profile of v0, /device:TPU:1, one launch (start us, length us, event | category | flops | bytes accessed | tf_op | source)
XLA Modules:
  0.0 370.7 jit_solution(4190907556177980599)
XLA Ops:
  6.5 0.0 copy-start
  6.5 0.0 all-reduce.3.cloned.1.call-start
  6.5 0.8 convert_element_type.2
  7.4 0.1 broadcast_in_dim.4
  7.5 0.1 reshape.16
  7.6 0.1 copy.22
  7.8 13.5 %fusion.7 = f32[512,56,56]{0,1,2:T(8,128)S(1)} fusion(f32[56,512,128]{2,1,0:T(8,128)} %param.7, f32[512,128]{1,0:T(8,128)S(1)} %copy.22, s32[128]{0:T(128)S(1)} %iota_add_fusion, s32[56]{0:T(128)} %param.9), kind=kOutput, calls=%fused_computation.7 | convolution fusion | flops 2469927936 | bytes 21365472 | tf_op jit(solution)/shard_map/wPp,pv->Pvw/dot_general | solution.py:24
  21.2 6.4 %copy.23 = f32[512,56,56]{0,2,1:T(8,128)} copy(f32[512,56,56]{0,1,2:T(8,128)S(1)} %fusion.7) | data formatting | bytes 12845056 | tf_op jit(solution)/shard_map/wPp,pv->Pvw/transpose | solution.py:24
  27.6 0.0 all-reduce.3.cloned.1.call-update
  27.6 0.0 copy-start.2
  27.6 0.0 copy-start.4
  27.6 0.0 copy-start.1
  27.7 0.2 all-gather.3.cloned.1.call-start
  27.9 143.9 %all-reduce.3.cloned.1.call-done = f32[512,3136]{0,1:T(8,128)} async-done(((f32[512,3136]{0,1:T(8,128)}), f32[512,3136]{0,1:T(8,128)}) %all-reduce.3.cloned.1.call-update) | async-done | bytes 6422544 | tf_op jit(solution)/shard_map/psum | solution.py:27
  171.8 0.0 copy-done
  171.8 8.6 %convolution_bitcast_fusion = f32[1,196,512]{2,1,0:T(8,128)} fusion(f32[512,3136]{0,1:T(8,128)} %all-reduce.3.cloned.1.call-done, f32[196,3136]{1,0:T(8,128)S(1)} %copy-done), kind=kOutput, calls=%fused_computation.8 | convolution fusion | flops 3776446464 | bytes 9282560 | tf_op jit(solution)/shard_map/dot_general | solution.py:28
  180.4 0.0 all-gather.3.cloned.1.call-update
  180.4 0.0 all-reduce.5.cloned.1.call-start
  180.5 0.0 copy-done.2
  180.5 0.1 copy.21
  180.6 0.0 copy-done.4
  180.6 0.1 pad_add_fusion
  180.7 0.0 copy-done.1
  180.7 63.3 %all-gather.3.cloned.1.call-done = f32[16,196,512]{2,1,0:T(8,128)} async-done(((f32[1,196,512]{2,1,0:T(8,128)}), f32[16,196,512]{2,1,0:T(8,128)}) %all-gather.3.cloned.1.call-update) | async-done | bytes 6422544 | tf_op jit(solution)/shard_map/all_gather | solution.py:29
  244.0 6.1 %reshape.20 = f32[3136,512]{1,0:T(8,128)} reshape(f32[16,196,512]{2,1,0:T(8,128)} %all-gather.3.cloned.1.call-done) | data formatting | bytes 12845056
  250.2 0.0 copy-start.3
  250.2 15.4 %fusion.11 = f32[128,56]{0,1:T(8,128)S(1)} fusion(f32[512,56,56]{0,2,1:T(8,128)} %bitcast.23, f32[56,512,128]{2,1,0:T(8,128)} %param.7, f32[512,128]{1,0:T(8,128)S(1)} %copy.22), kind=kOutput, calls=%fused_computation.11 | convolution fusion | flops 2469920768 | bytes 21393408 | tf_op jit(solution)/shard_map/uPp,Ptu->pt/dot_general | solution.py:30
  265.5 6.3 %psum.22 = f32[128,56]{0,1:T(8,128)S(1)} all-reduce(f32[128,56]{0,1:T(8,128)S(1)} %fusion.11), channel_id=1, replica_groups=mesh['orb'=16,'aux'=2] {'aux'}, use_global_device_ids=true, to_apply=%region_1.0 | all-reduce | flops 7168 | bytes 57344 | tf_op jit(solution)/shard_map/psum | solution.py:36
  271.8 0.0 copy-done.3
  271.8 0.3 convolution_add_fusion
  272.2 0.1 copy.25
  272.3 1.1 fusion.16
  273.4 0.0 all-reduce.5.cloned.1.call-update
  273.4 0.1 broadcast_compare_fusion
  273.5 88.9 %all-reduce.5.cloned.1.call-done = f32[256,256]{1,0:T(8,128)} async-done(((f32[256,256]{1,0:T(8,128)}), f32[256,256]{1,0:T(8,128)}) %all-reduce.5.cloned.1.call-update) | async-done | bytes 262160 | tf_op jit(solution)/shard_map/psum | solution.py:43
  362.3 1.9 fusion.10
  (4 shorter events, 0.0 us)
Async XLA Ops:
  6.5 165.2 %copy-start = (f32[196,3136]{1,0:T(8,128)S(1)}, f32[196,3136]{1,0:T(8,128)}, u32[]{:S(2)}) copy-start(f32[196,3136]{1,0:T(8,128)} %param.8) | copy-start | bytes 7375876
  6.5 165.2 %all-reduce.3.cloned.1.call-start = ((), (), s32[]{:S(2)}) async-start(), calls=%async_computation | async-start | bytes 12845056 | tf_op jit(solution)/shard_map/psum | solution.py:27
  27.6 152.8 %copy-start.2 = (f32[128,200]{0,1:T(8,128)S(1)}, f32[128,200]{0,1:T(8,128)}, u32[]{:S(2)}) copy-start(f32[128,200]{0,1:T(8,128)} %param.13) | copy-start | bytes 307204
  27.6 153.0 %copy-start.4 = (s32[56]{0:T(128)S(1)}, s32[56]{0:T(128)}, u32[]{:S(2)}) copy-start(s32[56]{0:T(128)} %param.9) | copy-start | bytes 676
  27.6 153.0 %copy-start.1 = (f32[128,256]{1,0:T(8,128)S(1)}, f32[128,256]{1,0:T(8,128)}, u32[]{:S(2)}) copy-start(f32[128,256]{1,0:T(8,128)} %param.12) | copy-start | bytes 393220
  27.7 216.4 %all-gather.3.cloned.1.call-start = ((), (), s32[]{:S(2)}) async-start(), calls=%async_computation.2 | async-start | bytes 6963200 | tf_op jit(solution)/shard_map/all_gather | solution.py:29
  180.4 181.9 %all-reduce.5.cloned.1.call-start = ((), (), s32[]{:S(2)}) async-start(), calls=%async_computation.1 | async-start | bytes 524288 | tf_op jit(solution)/shard_map/psum | solution.py:43
  250.2 21.7 %copy-start.3 = (f32[56,56]{1,0:T(8,128)S(1)}, f32[56,56]{1,0:T(8,128)}, u32[]{:S(2)}) copy-start(f32[56,56]{1,0:T(8,128)} %param.11) | copy-start | bytes 37636
Sparse Core Ops, SparseCore 0:
  27.7 143.9 all-reduce.2
  180.5 63.4 all-gather.2
  273.5 88.8 all-reduce.4
where the time goes:
time: 371 us
  waiting for transfers between devices  296 us (80%)
  matrix products  40.7 us (11%)
  between operations  13.2 us (4%)
  local copies, waits for them, and re-layouts  13 us (4%)
  blocking collectives  6.31 us (2%)
    psum x1, waiting for transfers between devices, shards(): pairs = lax.psum(partial_pairs, 'orb')  144 us
    psum x1, waiting for transfers between devices, shards(): occupied = lax.psum(jnp.dot(occ_pick.T, fock, precision=highest), 'orb')  88.9 us
    all_gather x1, waiting for transfers between devices, shards(): half = lax.all_gather(column_block, 'orb', axis=1, tiled=True)  63.3 us
    dot_general x1, matrix products, shards(): jnp.einsum('uPp,Ptu->pt', screened, half.reshape(slab_count, act_count, a...  15.4 us
    dot_general x1, matrix products, shards(): jnp.einsum('wPp,pv->Pvw', screened, active_pick, precision=highest)  13.5 us
    dot_general x1, matrix products, shards(): column_block = jnp.dot(pairs, pair_density.T, precision=highest)  8.61 us
  transfers between devices with their start and end apart: 3, of which 3 were waited for; matrix products, arithmetic and copies ran while one was open for 0% of the time, Pallas kernels for 0%

commit v1 on v0

--- a/solution.py
+++ b/solution.py
@@ -40,7 +40,7 @@
     )
     fock = jnp.concatenate([inactive_cols, active_cols], axis=1)
     occ_pick = (global_rows[:, None] == occ_index[None, :]).astype(jnp.float32)
-    occupied = lax.psum(jnp.dot(occ_pick.T, fock, precision=highest), "orb")
+    occupied = jnp.sum(lax.all_gather(jnp.dot(occ_pick.T, fock, precision=highest), "orb"), axis=0)
     fock_mine = lax.dynamic_slice_in_dim(fock, aux_offset, row_share, 0)
     pick_mine = lax.dynamic_slice_in_dim(occ_pick, aux_offset, row_share, 0)
     transposed = jnp.dot(pick_mine, occupied.T, precision=highest)

time: 371 us -> 334 us (0.900)
  waiting for transfers between devices: 296 us -> 258 us
    psum x1 -> x0, waiting for transfers between devices: 88.9 us -> none  [shards(): occupied = lax.psum(jnp.dot(occ_pick.T, fock, precision=highest), 'orb')]
    all_gather x0 -> x1, waiting for transfers between devices: none -> 50.3 us  [shards(): lax.all_gather(jnp.dot(occ_pick.T, fock, precision=highest), 'orb')]
where the time goes in v1:
time: 334 us
  waiting for transfers between devices  258 us (77%)
  matrix products  39.8 us (12%)
  between operations  13.2 us (4%)
  local copies, waits for them, and re-layouts  13 us (4%)
  blocking collectives  6.31 us (2%)
  other arithmetic  3.51 us (1%)
    psum x1, waiting for transfers between devices, shards(): pairs = lax.psum(partial_pairs, 'orb')  144 us
    all_gather x1, waiting for transfers between devices, shards(): half = lax.all_gather(column_block, 'orb', axis=1, tiled=True)  63.4 us
    all_gather x1, waiting for transfers between devices, shards(): lax.all_gather(jnp.dot(occ_pick.T, fock, precision=highest), 'orb')  50.3 us
    dot_general x1, matrix products, shards(): jnp.einsum('uPp,Ptu->pt', screened, half.reshape(slab_count, act_count, a...  15.4 us
    dot_general x1, matrix products, shards(): jnp.einsum('wPp,pv->Pvw', screened, active_pick, precision=highest)  13.5 us
    dot_general x1, matrix products, shards(): column_block = jnp.dot(pairs, pair_density.T, precision=highest)  8.61 us
  transfers between devices with their start and end apart: 3, of which 3 were waited for; matrix products, arithmetic and copies ran while one was open for 0% of the time, Pallas kernels for 0%

profile of v1, /device:TPU:1, one launch (start us, length us, event | category | flops | bytes accessed | tf_op | source)
XLA Modules:
  0.0 333.7 jit_solution(12978675800703933862)
XLA Ops:
  6.5 0.0 copy-start
  6.5 0.0 all-reduce.2.cloned.1.call-start
  6.5 0.8 convert_element_type.2
  7.4 0.1 broadcast_in_dim.4
  7.5 0.1 reshape.16
  7.6 0.1 copy.22
  7.8 13.5 %fusion.7 = f32[512,56,56]{0,1,2:T(8,128)S(1)} fusion(f32[56,512,128]{2,1,0:T(8,128)} %param.7, f32[512,128]{1,0:T(8,128)S(1)} %copy.22, s32[128]{0:T(128)S(1)} %iota_add_fusion, s32[56]{0:T(128)} %param.9), kind=kOutput, calls=%fused_computation.7 | convolution fusion | flops 2469927936 | bytes 21365472 | tf_op jit(solution)/shard_map/wPp,pv->Pvw/dot_general | solution.py:24
  21.2 6.4 %copy.23 = f32[512,56,56]{0,2,1:T(8,128)} copy(f32[512,56,56]{0,1,2:T(8,128)S(1)} %fusion.7) | data formatting | bytes 12845056 | tf_op jit(solution)/shard_map/wPp,pv->Pvw/transpose | solution.py:24
  27.6 0.0 all-reduce.2.cloned.1.call-update
  27.6 0.0 copy-start.2
  27.6 0.0 copy-start.4
  27.6 0.0 copy-start.1
  27.7 0.2 all-gather.7.cloned.1.call-start
  27.9 143.9 %all-reduce.2.cloned.1.call-done = f32[512,3136]{0,1:T(8,128)} async-done(((f32[512,3136]{0,1:T(8,128)}), f32[512,3136]{0,1:T(8,128)}) %all-reduce.2.cloned.1.call-update) | async-done | bytes 6422544 | tf_op jit(solution)/shard_map/psum | solution.py:27
  171.8 0.0 copy-done
  171.8 8.6 %convolution_bitcast_fusion = f32[1,196,512]{2,1,0:T(8,128)} fusion(f32[512,3136]{0,1:T(8,128)} %all-reduce.2.cloned.1.call-done, f32[196,3136]{1,0:T(8,128)S(1)} %copy-done), kind=kOutput, calls=%fused_computation.8 | convolution fusion | flops 3776446464 | bytes 9282560 | tf_op jit(solution)/shard_map/dot_general | solution.py:28
  180.4 0.0 all-gather.7.cloned.1.call-update
  180.4 0.0 all-gather.5.cloned.1.call-start
  180.5 0.0 copy-done.2
  180.5 0.1 copy.21
  180.6 0.0 copy-done.4
  180.6 0.1 pad_add_fusion
  180.7 0.0 copy-done.1
  180.7 63.4 %all-gather.7.cloned.1.call-done = f32[16,196,512]{2,1,0:T(8,128)} async-done(((f32[1,196,512]{2,1,0:T(8,128)}), f32[16,196,512]{2,1,0:T(8,128)}) %all-gather.7.cloned.1.call-update) | async-done | bytes 6422544 | tf_op jit(solution)/shard_map/all_gather | solution.py:29
  244.0 6.1 %reshape.21 = f32[3136,512]{1,0:T(8,128)} reshape(f32[16,196,512]{2,1,0:T(8,128)} %all-gather.7.cloned.1.call-done) | data formatting | bytes 12845056
  250.2 0.0 copy-start.3
  250.2 15.4 %fusion.11 = f32[128,56]{0,1:T(8,128)S(1)} fusion(f32[512,56,56]{0,2,1:T(8,128)} %bitcast.24, f32[56,512,128]{2,1,0:T(8,128)} %param.7, f32[512,128]{1,0:T(8,128)S(1)} %copy.22), kind=kOutput, calls=%fused_computation.11 | convolution fusion | flops 2469920768 | bytes 21393408 | tf_op jit(solution)/shard_map/uPp,Ptu->pt/dot_general | solution.py:30
  265.5 6.3 %psum.15 = f32[128,56]{0,1:T(8,128)S(1)} all-reduce(f32[128,56]{0,1:T(8,128)S(1)} %fusion.11), channel_id=1, replica_groups=mesh['orb'=16,'aux'=2] {'aux'}, use_global_device_ids=true, to_apply=%region_1.0 | all-reduce | flops 7168 | bytes 57344 | tf_op jit(solution)/shard_map/psum | solution.py:36
  271.8 0.0 copy-done.3
  271.8 0.3 convolution_add_fusion
  272.2 0.1 copy.25
  272.3 1.1 fusion.16
  273.4 0.0 all-gather.5.cloned.1.call-update
  273.4 0.1 broadcast_compare_fusion
  273.5 50.3 %all-gather.5.cloned.1.call-done = f32[4096,256]{1,0:T(8,128)} async-done(((f32[256,256]{1,0:T(8,128)}), f32[4096,256]{1,0:T(8,128)}) %all-gather.5.cloned.1.call-update) | async-done | bytes 4194320 | tf_op jit(solution)/shard_map/all_gather | solution.py:43
  323.8 2.5 reduce_sum.9
  326.3 0.9 fusion.10
  (4 shorter events, 0.0 us)
Async XLA Ops:
  6.5 165.2 %copy-start = (f32[196,3136]{1,0:T(8,128)S(1)}, f32[196,3136]{1,0:T(8,128)}, u32[]{:S(2)}) copy-start(f32[196,3136]{1,0:T(8,128)} %param.8) | copy-start | bytes 7375876
  6.5 165.2 %all-reduce.2.cloned.1.call-start = ((), (), s32[]{:S(2)}) async-start(), calls=%async_computation | async-start | bytes 12845056 | tf_op jit(solution)/shard_map/psum | solution.py:27
  27.6 152.8 %copy-start.2 = (f32[128,200]{0,1:T(8,128)S(1)}, f32[128,200]{0,1:T(8,128)}, u32[]{:S(2)}) copy-start(f32[128,200]{0,1:T(8,128)} %param.13) | copy-start | bytes 307204
  27.6 153.0 %copy-start.4 = (s32[56]{0:T(128)S(1)}, s32[56]{0:T(128)}, u32[]{:S(2)}) copy-start(s32[56]{0:T(128)} %param.9) | copy-start | bytes 676
  27.6 153.0 %copy-start.1 = (f32[128,256]{1,0:T(8,128)S(1)}, f32[128,256]{1,0:T(8,128)}, u32[]{:S(2)}) copy-start(f32[128,256]{1,0:T(8,128)} %param.12) | copy-start | bytes 393220
  27.7 216.4 %all-gather.7.cloned.1.call-start = ((), (), s32[]{:S(2)}) async-start(), calls=%async_computation.2 | async-start | bytes 6963200 | tf_op jit(solution)/shard_map/all_gather | solution.py:29
  180.4 143.4 %all-gather.5.cloned.1.call-start = ((), (), s32[]{:S(2)}) async-start(), calls=%async_computation.1 | async-start | bytes 4456448 | tf_op jit(solution)/shard_map/all_gather | solution.py:43
  250.2 21.7 %copy-start.3 = (f32[56,56]{1,0:T(8,128)S(1)}, f32[56,56]{1,0:T(8,128)}, u32[]{:S(2)}) copy-start(f32[56,56]{1,0:T(8,128)} %param.11) | copy-start | bytes 37636
Sparse Core Ops, SparseCore 0:
  27.7 143.9 all-reduce.1
  180.5 63.4 all-gather.6
  273.5 50.2 all-gather.4
